TPU v7x, 32 devices: a whole 2x2x4 slice. The times are simulated.
32 devices in a mesh: parts: 1, chan: 16 (over z, y, core), tm: 2 (over x), freq: 1.
Axes of the slice: x: 2, y: 2, z: 4, core: 2. Of those that a mesh axis runs over, the one named last changes fastest.
Arguments:
- spectra: bfloat16 [2, 512, 16, 2048], P(None, 'freq', 'tm', ('parts', 'chan')), may hold values from -6 to 6
- owners: int32 [4], P('parts'), may hold values from 0 to 15
- source_rows: int32 [4, 16], P('parts'), may hold values from 0 to 127
Outputs:
- correlations: float32 [4, 16, 2048, 128], P(None, ('tm', 'freq'), ('parts', 'chan'))
All inputs are finite; a program needn't handle non-finite values.
Results may differ from a plain program's by a relative error of at most 0.0037.
Values may be sent and summed in bfloat16 or wider, within the bound.
A program may use at most 64 MiB of HBM per device.

v0:
```python
import jax
import jax.numpy as jnp
from jax import lax
from jax.sharding import PartitionSpec as P

WINDOW_LEN = 4096
FIRST_BIN = 64
LAGS = 128
WATER = 0.5


def whiten(block):
    values = block.astype(jnp.float32)
    size = jnp.sqrt(values[0] * values[0] + values[1] * values[1]) + WATER
    return (values / size[None]).astype(jnp.bfloat16)


def make_tables(first_bin, count):
    bins = first_bin + jnp.arange(count, dtype=jnp.int32)
    shifts = jnp.arange(LAGS, dtype=jnp.int32) - LAGS // 2
    phase = jnp.mod(bins[:, None] * shifts[None, :], WINDOW_LEN).astype(jnp.float32)
    angle = phase * (2.0 * 3.141592653589793 / WINDOW_LEN)
    return jnp.stack([jnp.cos(angle), -jnp.sin(angle)])


def per_device(spectra, owners, source_rows):
    whitened = whiten(spectra)
    bins, wins, chans = whitened.shape[1:]
    steps, per_step = source_rows.shape
    total = steps * per_step
    scale = 1.0 / (wins * lax.axis_size("tm"))
    first_bin = FIRST_BIN + lax.axis_index("freq") * bins
    tables = (make_tables(first_bin, bins) * scale).astype(jnp.bfloat16)
    mine = owners == lax.axis_index("chan")
    rows = jnp.where(mine[:, None], source_rows, -1).reshape(total)
    pick = (rows[:, None] == jnp.arange(chans)[None, :]).astype(jnp.bfloat16)
    block = jnp.einsum("kfwc,sc->kfsw", whitened, pick, preferred_element_type=jnp.bfloat16)
    block = lax.psum(block, "chan")
    flipped = jnp.stack([block, jnp.stack([-block[1], block[0]])])
    cross = jnp.einsum("okfsw,kfwc->ofsc", flipped, whitened, preferred_element_type=jnp.float32)
    cross = cross.astype(jnp.bfloat16)
    lags = jnp.einsum("ofsc,ofl->scl", cross, tables, preferred_element_type=jnp.float32)
    lags = lags.astype(jnp.bfloat16).reshape(steps, per_step, chans, LAGS)
    lags = lax.psum_scatter(lags, ("tm", "freq"), scatter_dimension=1, tiled=True)
    return lags.astype(jnp.float32)


def solution(mesh):
    placed = (P(None, "freq", "tm", ("parts", "chan")), P("parts"), P("parts", None))
    return jax.shard_map(
        per_device,
        mesh=mesh,
        in_specs=placed,
        out_specs=P(None, ("tm", "freq"), ("parts", "chan"), None),
        check_vma=False,
    )
```

profile of v0, /device:TPU:0, one launch (start us, length us, event | category | flops | bytes accessed | tf_op | source)
XLA Modules:
  0.0 211.4 jit_solution(3605232848180694408)
XLA Ops:
  6.5 0.0 all-reduce.2.cloned.1.call-start
  6.5 1.9 convert_element_type.38
  8.4 0.0 copy-start
  8.4 0.7 fusion.8
  9.2 0.0 copy-start.1
  9.2 1.3 copy-done.1
  10.5 0.0 copy-done
  10.5 0.0 copy-start.4
  10.5 1.8 divide_convert_fusion
  12.3 0.0 copy-done.4
  12.3 0.0 copy-done.3
  12.3 0.1 broadcast_select_fusion
  12.4 0.1 eq.25
  12.5 3.5 %fusion.13 = bf16[2,512,64,8]{1,2,3,0:T(8,128)(2,1)} fusion(bf16[2,512,8,128]{3,2,1,0:T(8,128)(2,1)} %divide_convert_fusion, s32[64]{0:T(128)S(1)} %eq.25), kind=kOutput, calls=%fused_computation.17 | convolution fusion | flops 134225920 | bytes 3145984 | tf_op jit(solution)/shard_map/kfwc,sc->kfsw/dot_general | solution.py:37
  16.0 0.0 all-reduce.2.cloned.1.call-update
  16.0 0.0 reduce-scatter.5.cloned.1.call-start
  16.1 1.1 fusion.23
  17.2 95.4 %all-reduce.2.cloned.1.call-done = bf16[2,512,64,8]{1,2,3,0:T(8,128)(2,1)} async-done(((bf16[2,512,64,8]{1,2,3,0:T(8,128)(2,1)}), bf16[2,512,64,8]{1,2,3,0:T(8,128)(2,1)}) %all-reduce.2.cloned.1.call-update) | async-done | bytes 1048592 | tf_op jit(solution)/shard_map/psum | solution.py:38
  112.6 1.4 slice_negate_fusion
  114.0 0.1 maximum_bitcast_fusion
  114.1 0.1 copy-done.2
  114.2 1.5 pad_maximum_fusion
  115.7 7.4 %copy.8 = bf16[2,2,512,64,8]{3,4,1,0,2:T(8,128)(2,1)} copy(bf16[2,2,512,64,8]{2,3,4,1,0:T(8,128)(2,1)} %pad_maximum_fusion) | data formatting | bytes 4194304 | tf_op jit(solution)/shard_map/stack | solution.py:39
  123.1 10.0 %fusion.9 = bf16[512,128,2,64,1]{1,3,4,2,0:T(8,128)(2,1)} fusion(bf16[2,2,512,64,8]{3,4,1,0,2:T(8,128)(2,1)} %copy.8, f32[512,8,128]{2,1,0:T(8,128)} %copy-done.1, bf16[2,512,8,128]{3,2,1,0:T(8,128)(2,1)S(1)} %copy-done), kind=kOutput, calls=%fused_computation.13 | convolution fusion | flops 271581184 | bytes 23068672 | tf_op jit(solution)/shard_map/okfsw,kfwc->ofsc/dot_general | solution.py:40
  133.1 24.1 %copy.9 = bf16[512,128,2,64,1]{0,1,2,3,4:T(8,128)(2,1)} copy(bf16[512,128,2,64,1]{1,3,4,2,0:T(8,128)(2,1)} %fusion.9) | data formatting | bytes 33554432 | tf_op jit(solution)/shard_map/okfsw,kfwc->ofsc/dot_general | solution.py:40
  157.2 10.3 %bitcast_convert_fusion.1 = bf16[64,128,128]{2,1,0:T(8,128)(2,1)S(1)} fusion(bf16[512,128,2,64,1]{0,1,2,3,4:T(8,128)(2,1)} %copy.9, f32[1,512,128]{2,1,0:T(8,128)S(1)} %get-tuple-element.8, f32[1,512,128]{2,1,0:T(8,128)S(1)} %get-tuple-element.7), kind=kOutput, calls=%fused_computation.3 | convolution fusion | flops 2148925440 | bytes 19398656 | tf_op jit(solution)/shard_map/ofsc,ofl->scl/dot_general | solution.py:42
  167.5 0.2 copy.11
  167.8 2.7 %copy.23 = bf16[2,8,512,128]{3,1,2,0:T(8,128)(2,1)} copy(bf16[2,8,512,128]{3,2,1,0:T(8,128)(2,1)S(1)} %bitcast.50) | data formatting | bytes 4194304
  170.4 0.0 reduce-scatter.5.cloned.1.call-update
  170.5 31.1 %reduce-scatter.5.cloned.1.call-done = bf16[8,65536]{1,0:T(8,128)(2,1)} async-done(((bf16[16,65536]{1,0:T(8,128)(2,1)}), bf16[8,65536]{1,0:T(8,128)(2,1)}) %reduce-scatter.5.cloned.1.call-update) | async-done | bytes 1048592
  201.6 1.4 copy.14
  203.0 1.6 copy_convert_fusion
  (5 shorter events, 0.0 us)
Async XLA Ops:
  6.5 106.1 %all-reduce.2.cloned.1.call-start = ((), (), s32[]{:S(2)}) async-start(), calls=%async_computation.1 | async-start | bytes 2097152 | tf_op jit(solution)/shard_map/psum | solution.py:38
  8.4 2.1 copy-start
  9.2 1.3 copy-start.1
  10.5 1.8 copy-start.4
  10.5 1.8 copy-start.3
  16.0 185.6 %reduce-scatter.5.cloned.1.call-start = ((), (), s32[]{:S(2)}) async-start(), calls=%async_computation.2 | async-start | bytes 3145728
  112.6 1.5 copy-start.2
Sparse Core Ops, SparseCore 0:
  16.2 96.4 all-reduce.1
  170.6 30.9 reduce-scatter.4
where the time goes:
time: 212 us; the launch traced here: 211 us
  waiting for transfers between devices  127 us (60%)
  local copies, waits for them, and re-layouts  37.3 us (18%)
  matrix products  23.8 us (11%)
  between operations  13.5 us (6%)
  other arithmetic  10.1 us (5%)
    psum x1, waiting for transfers between devices, per_device(): block = lax.psum(block, 'chan')  95.4 us
    unnamed x3, waiting for transfers between devices  31.2 us
    dot_general x1, local copies, waits for them, and re-layouts, per_device(): jnp.einsum('okfsw,kfwc->ofsc', flipped, whitened, preferred_element_type=...  24.1 us
    dot_general x1, matrix products, per_device(): jnp.einsum('ofsc,ofl->scl', cross, tables, preferred_element_type=jnp.flo...  10.3 us
    dot_general x1, matrix products, per_device(): jnp.einsum('okfsw,kfwc->ofsc', flipped, whitened, preferred_element_type=...  10 us
    another operation x1, local copies, waits for them, and re-layouts, per_device(): flipped = jnp.stack([block, jnp.stack([-block[1], block[0]])])  7.42 us
    unnamed x13, local copies, waits for them, and re-layouts  5.68 us
  transfers between devices with their start and end apart: 2, of which 2 were waited for; matrix products, arithmetic and copies ran while one was open for 1% of the time, Pallas kernels for 0%

commit v1 on v0

v1 whole, which is shorter than its diff:
```python
import functools

import jax
import jax.numpy as jnp
import numpy as np
from jax import lax
from jax.experimental import pallas as pl
from jax.experimental.pallas import tpu as pltpu
from jax.sharding import PartitionSpec as P

WINDOW_LEN = 4096
FIRST_BIN = 64
LAGS = 128
WATER = 0.5
AXES = ("parts", "chan", "tm", "freq")
MESH = pl.DeviceIdType.MESH


def table(count, scale):
    bins = FIRST_BIN + np.arange(count)
    shifts = np.arange(LAGS) - LAGS // 2
    angle = np.mod(shifts[:, None] * bins[None, :], WINDOW_LEN) * (2.0 * np.pi / WINDOW_LEN)
    return np.stack([np.cos(angle), -np.sin(angle)], axis=1) * scale


def kernel(sizes, spec_ref, pick_ref, table_ref, out_ref,
           wh, held, got1, got2, got_full, whole, cross, own, send, recv,
           bsend, brecv, xsend, xrecv):
    steps, per_step, bins, wins, chans, n_chan, n_tm, n_freq = sizes
    group = 128 // wins
    lanes = bins * wins
    half = lanes // 2
    peers = n_tm * n_freq
    per = per_step // peers
    part, me = lax.axis_index("parts"), lax.axis_index("chan")
    tm, fq = lax.axis_index("tm"), lax.axis_index("freq")
    rank = tm * n_freq + fq
    bit0, bit1 = me % 2, (me // 2) % 2
    dists = []
    while 2 ** len(dists) < n_chan:
        dists.append(2 ** len(dists))
    far = dists[2:]
    stages = [1, 2] + far + [2, 1]

    def along(d):
        return (part, me + d * (1 - 2 * ((me // d) % 2)), tm, fq)

    def peer(p):
        other = (rank + p) % peers
        return (part, me, other // n_freq, other % n_freq), other

    barrier = pltpu.get_barrier_semaphore()
    for d in dists:
        pl.semaphore_signal(barrier, inc=1, device_id=along(d), device_id_type=MESH)
    for p in range(1, peers):
        pl.semaphore_signal(barrier, inc=1, device_id=peer(p)[0], device_id_type=MESH)

    rows = 256

    def whiten(i, carry):
        at = pl.ds(pl.multiple_of(i * rows, rows), rows)
        re = spec_ref[0, at, :].astype(jnp.float32)
        im = spec_ref[1, at, :].astype(jnp.float32)
        size = jnp.sqrt(re * re + im * im) + WATER
        wh[0, at, :] = (re / size).astype(jnp.bfloat16)
        wh[1, at, :] = (im / size).astype(jnp.bfloat16)
        return carry

    lax.fori_loop(0, lanes // rows, whiten, 0)

    for k in range(2):
        for h in range(2):
            def choose(i, carry):
                at = pl.ds(pl.multiple_of(h * half + i * rows, rows), rows)
                got = lax.dot_general(pick_ref[...], wh[k, at, :], (((1,), (1,)), ((), ())),
                                      preferred_element_type=jnp.float32).astype(jnp.bfloat16)
                to = pl.ds(pl.multiple_of(i * rows, rows), rows)
                for t in range(steps):
                    held[t, 2 * k + h, :, to] = got[t * per_step:(t + 1) * per_step]
                return carry

            lax.fori_loop(0, half // rows, choose, 0)

    pl.semaphore_wait(barrier, len(dists) + peers - 1)

    keep = 2 * bit0 + bit1
    last = len(stages) - 1

    def copy(t, st):
        d = stages[st]
        if st == 0:
            src, dst = held.at[t, pl.ds(2 * (1 - bit0), 2)], got1.at[t]
        elif st == 1:
            src, dst = held.at[t, 2 * bit0 + 1 - bit1], got2.at[t]
        elif st < last - 1:
            src, dst = held.at[t, keep], got_full.at[t, st - 2]
        elif st == last - 1:
            src = dst = whole.at[t, keep]
        else:
            src = dst = whole.at[t, pl.ds(2 * bit0, 2)]
        return pltpu.make_async_remote_copy(
            src_ref=src, dst_ref=dst, send_sem=bsend.at[t, st], recv_sem=brecv.at[t, st],
            device_id=along(d), device_id_type=MESH)

    def finish(t, st):
        copy(t, st).wait()
        if st == 0:
            for q in range(2):
                held[t, 2 * bit0 + q] = held[t, 2 * bit0 + q] + got1[t, q]
        elif st == 1:
            held[t, keep] = held[t, keep] + got2[t]
        elif st < last - 1:
            held[t, keep] = held[t, keep] + got_full[t, st - 2]
        if st == last - 2:
            whole[t, keep] = held[t, keep]

    lane = lax.broadcasted_iota(jnp.int32, (1, group, 128), 2)
    bin_of = lax.broadcasted_iota(jnp.int32, (1, group, 128), 1)
    mine = (lane // wins) == bin_of

    def spread(x):
        wide = jnp.where(mine, x[:, None, :], 0.0)
        return wide.reshape(per_step * group, 128).astype(jnp.bfloat16)

    def exchange(t, p):
        return pltpu.make_async_remote_copy(
            src_ref=send.at[t, p - 1], dst_ref=recv.at[t, p - 1],
            send_sem=xsend.at[t, p - 1], recv_sem=xrecv.at[t, p - 1],
            device_id=peer(p)[0], device_id_type=MESH)

    def compute(t):
        for h in range(2):
            def one(i, carry):
                g = pl.multiple_of(i * 128, 128)
                re = whole[t, h, :, pl.ds(g, 128)].astype(jnp.float32)
                im = whole[t, 2 + h, :, pl.ds(g, 128)].astype(jnp.float32)
                wre, wim = spread(re), spread(im)
                at = pl.ds(pl.multiple_of(h * half + i * 128, 128), 128)
                right = jnp.concatenate([wh[0, at, :], wh[1, at, :]], axis=0)
                real = jnp.dot(jnp.concatenate([wre, wim], axis=1), right, preferred_element_type=jnp.float32)
                imag = jnp.dot(jnp.concatenate([-wim, wre], axis=1), right, preferred_element_type=jnp.float32)
                first = h * (bins // 2) + i * group
                for o, value in enumerate((real, imag)):
                    to = pl.ds(pl.multiple_of(o * bins + first, group), group)
                    cross[:, to, :] = value.reshape(per_step, group, chans).astype(jnp.bfloat16)
                return carry

            lax.fori_loop(0, half // 128, one, 0)

        def lag_pair(s):
            both = jnp.concatenate([cross[s], cross[s + 1]], axis=1)
            return jnp.dot(table_ref[...], both, preferred_element_type=jnp.float32)

        for p in range(1, peers):
            other = peer(p)[1]

            def away(i, carry):
                got = lag_pair(other * per + 2 * i).astype(jnp.bfloat16)
                send[t, p - 1, 2 * i] = got[:, :chans]
                send[t, p - 1, 2 * i + 1] = got[:, chans:]
                return carry

            lax.fori_loop(0, per // 2, away, 0)
            exchange(t, p).start()

        def home(i, carry):
            got = lag_pair(rank * per + 2 * i)
            own[t, 2 * i] = got[:, :chans]
            own[t, 2 * i + 1] = got[:, chans:]
            return carry

        lax.fori_loop(0, per // 2, home, 0)

    def close(t):
        for p in range(1, peers):
            exchange(t, p).wait()

        def one(j, carry):
            value = own[t, j]
            for p in range(1, peers):
                value = value + recv[t, p - 1, j].astype(jnp.float32)
            out_ref[t, j] = value.T
            return carry

        lax.fori_loop(0, per, one, 0)

    count = len(stages)
    for t in range(steps):
        copy(t, 0).start()
    for wave in range(steps + count + 1):
        for t in range(steps):
            st = wave - t
            if 0 <= st < count:
                finish(t, st)
                if st + 1 < count:
                    copy(t, st + 1).start()
            elif st == count:
                compute(t)
            elif st == count + 1:
                close(t)


def per_device(spectra, owners, source_rows):
    _, bins, wins, chans = spectra.shape
    steps, per_step = source_rows.shape
    n_chan, n_tm, n_freq = (lax.axis_size(a) for a in AXES[1:])
    peers = n_tm * n_freq
    per = per_step // peers
    lanes = bins * wins
    full = jnp.asarray(table(bins * n_freq, 1.0 / (wins * n_tm)).astype(jnp.bfloat16))
    tables = lax.dynamic_slice_in_dim(full, lax.axis_index("freq") * bins, bins, 2) if n_freq > 1 else full
    tables = tables.reshape(LAGS, 2 * bins)
    mine = owners == lax.axis_index("chan")
    rows = jnp.where(mine[:, None], source_rows, -1).reshape(-1)
    pick = (rows[:, None] == jnp.arange(chans)[None, :]).astype(jnp.bfloat16)
    far = max(n_chan.bit_length() - 3, 1)
    count = n_chan.bit_length() + 1
    sizes = (steps, per_step, bins, wins, chans, n_chan, n_tm, n_freq)
    bf16, f32 = jnp.bfloat16, jnp.float32
    quarter = (per_step, lanes // 2)
    vmem = pl.BlockSpec(memory_space=pltpu.VMEM)
    return pl.pallas_call(
        functools.partial(kernel, sizes),
        out_shape=jax.ShapeDtypeStruct((steps, per, chans, LAGS), f32),
        in_specs=[vmem] * 3,
        out_specs=vmem,
        scratch_shapes=[
            pltpu.VMEM((2, lanes, chans), bf16),
            pltpu.VMEM((steps, 4) + quarter, bf16),
            pltpu.VMEM((steps, 2) + quarter, bf16),
            pltpu.VMEM((steps,) + quarter, bf16),
            pltpu.VMEM((steps, far) + quarter, bf16),
            pltpu.VMEM((steps, 4) + quarter, bf16),
            pltpu.VMEM((per_step, 2 * bins, chans), bf16),
            pltpu.VMEM((steps, per, LAGS, chans), f32),
            pltpu.VMEM((steps, peers - 1, per, LAGS, chans), bf16),
            pltpu.VMEM((steps, peers - 1, per, LAGS, chans), bf16),
            pltpu.SemaphoreType.DMA((steps, count)),
            pltpu.SemaphoreType.DMA((steps, count)),
            pltpu.SemaphoreType.DMA((steps, peers - 1)),
            pltpu.SemaphoreType.DMA((steps, peers - 1)),
        ],
        compiler_params=pltpu.CompilerParams(collective_id=0, has_side_effects=True),
    )(spectra.reshape(2, lanes, chans), pick, tables)


def solution(mesh):
    placed = (P(None, "freq", "tm", ("parts", "chan")), P("parts"), P("parts", None))
    return jax.shard_map(
        per_device,
        mesh=mesh,
        in_specs=placed,
        out_specs=P(None, ("tm", "freq"), ("parts", "chan"), None),
        check_vma=False,
    )
```

time: 212 us -> 98.4 us (0.46)
  waiting for transfers between devices: 127 us -> 0 us
  Pallas kernels: 0 us -> 92.8 us
  local copies, waits for them, and re-layouts: 37.3 us -> 3.22 us
  matrix products: 23.8 us -> 0 us
  between operations: 13.5 us -> 0.01 us
  other arithmetic: 10.1 us -> 2.1 us
    psum x1 -> x0, waiting for transfers between devices: 95.4 us -> none  [per_device(): block = lax.psum(block, 'chan')]
    pallas_call x0 -> x1, Pallas kernels: none -> 92.8 us  [per_device(): pl.pallas_call(functools.partial(kernel, sizes), out_shape=jax.ShapeDtype...]
    unnamed x3 -> x0, waiting for transfers between devices: 31.2 us -> none
    dot_general x1 -> x0, local copies, waits for them, and re-layouts: 24.1 us -> none  [per_device(): jnp.einsum('okfsw,kfwc->ofsc', flipped, whitened, preferred_element_type=...]
    dot_general x3 -> x0, matrix products: 23.8 us -> none  [the longest x1 10.3 us: per_device(): jnp.einsum('ofsc,ofl->scl', cross, tables, preferred_element_type=jnp.flo...]
    another operation x1 -> x0, local copies, waits for them, and re-layouts: 7.42 us -> none  [per_device(): flipped = jnp.stack([block, jnp.stack([-block[1], block[0]])])]
    convert_element_type x3 -> x1, other arithmetic: 5.24 us -> 0.69 us  [per_device(): pick = (rows[:, None] == jnp.arange(chans)[None, :]).astype(jnp.bfloat16)]
    unnamed x13 -> x1, local copies, waits for them, and re-layouts: 5.68 us -> 3.14 us
  transfers between devices with their start and end apart: 2 -> 0, of which waited for: 2 -> 0; matrix products, arithmetic and copies ran while one was open for 1% -> 0% of each run, Pallas kernels for 0% -> 0%
where the time goes in v1:
time: 98.4 us; the launch traced here: 98.2 us
  Pallas kernels  92.8 us (94%)
  local copies, waits for them, and re-layouts  3.22 us (3%)
  other arithmetic  2.1 us (2%)
    pallas_call x1, Pallas kernels, per_device(): pl.pallas_call(functools.partial(kernel, sizes), out_shape=jax.ShapeDtype...  92.8 us
    unnamed x1, local copies, waits for them, and re-layouts  3.14 us

profile of v1, /device:TPU:0, one launch (start us, length us, event | category | flops | bytes accessed | tf_op | source)
XLA Modules:
  0.0 98.2 jit_solution(17743800158330778699)
XLA Ops:
  0.0 0.7 broadcast_compare_fusion
  0.7 0.8 broadcast_select_fusion
  1.4 0.1 eq.23
  1.5 0.7 fusion.pick_ref
  2.2 92.8 %shard_map.46 = f32[4,8,128,128]{3,2,1,0:T(8,128)} custom-call(bf16[2,4096,128]{2,1,0:T(8,128)(2,1)} %bitcast.1, bf16[64,128]{1,0:T(8,128)(2,1)} %fusion.pick_ref, bf16[128,1024]{1,0:T(8,128)(2,1)} %constant.11.table_ref), custom_call_target="tpu_custom_call" | custom-call | tf_op jit(solution)/shard_map/pallas_call | solution.py:222
  95.0 3.1 %copy.6 = f32[4,8,128,128]{3,2,1,0:T(8,128)} copy(f32[4,8,128,128]{3,2,1,0:T(8,128)} %shard_map.46) | data formatting | bytes 4194304

commit v2 on v1

v2 whole, which is shorter than its diff:
```python
import functools

import jax
import jax.numpy as jnp
import numpy as np
from jax import lax
from jax.experimental import pallas as pl
from jax.experimental.pallas import tpu as pltpu
from jax.sharding import PartitionSpec as P

WINDOW_LEN = 4096
FIRST_BIN = 64
LAGS = 128
WATER = 0.5
AXES = ("parts", "chan", "tm", "freq")
MESH = pl.DeviceIdType.MESH


def table(count, scale):
    bins = FIRST_BIN + np.arange(count)
    shifts = np.arange(LAGS) - LAGS // 2
    angle = np.mod(shifts[:, None] * bins[None, :], WINDOW_LEN) * (2.0 * np.pi / WINDOW_LEN)
    return np.stack([np.cos(angle), -np.sin(angle)], axis=1) * scale


def layout(steps, per_step, peers):
    block = steps * (per_step // peers)
    piece = max(min(per_step, block) // 2, 2)
    return block, piece, (peers - 1) * block // piece


def kernel(sizes, owner_ref, row_ref, spec_ref, table_ref, out_ref,
           pick, right, held, got1, got2, got_full, whole, cross, own, send, recv,
           bsend, brecv, xsend, xrecv):
    steps, per_step, bins, wins, chans, n_chan, n_tm, n_freq = sizes
    group = 128 // wins
    lanes = bins * wins
    half = lanes // 2
    groups = lanes // 128
    peers = n_tm * n_freq
    per = per_step // peers
    block, piece, sends = layout(steps, per_step, peers)
    part, me = lax.axis_index("parts"), lax.axis_index("chan")
    tm, fq = lax.axis_index("tm"), lax.axis_index("freq")
    rank = tm * n_freq + fq
    bit0, bit1 = me % 2, (me // 2) % 2
    dists = []
    while 2 ** len(dists) < n_chan:
        dists.append(2 ** len(dists))
    far = dists[2:]
    stages = [1, 2] + far + [2, 1]

    def along(d):
        return (part, me + d * (1 - 2 * ((me // d) % 2)), tm, fq)

    def peer(p):
        other = (rank + p) % peers
        return (part, me, other // n_freq, other % n_freq)

    barrier = pltpu.get_barrier_semaphore()
    for d in dists:
        pl.semaphore_signal(barrier, inc=1, device_id=along(d), device_id_type=MESH)
    for p in range(1, peers):
        pl.semaphore_signal(barrier, inc=1, device_id=peer(p), device_id_type=MESH)

    channel = lax.broadcasted_iota(jnp.int32, (1, chans), 1)
    for p in range(1, peers + 1):
        for t in range(steps):
            held_here = owner_ref[t] == me
            for j in range(per):
                row = jnp.where(held_here, row_ref[t, ((rank + p) % peers) * per + j], -1)
                at = (p - 1) * block + t * per + j
                pick[pl.ds(at, 1), :] = (channel == row).astype(jnp.float32)
    chosen = pick[...].astype(jnp.bfloat16)

    def prepare(h, i):
        g = h * (groups // 2) + i
        at = pl.ds(pl.multiple_of(g * 128, 128), 128)
        re = spec_ref[0, at, :].astype(jnp.float32)
        im = spec_ref[1, at, :].astype(jnp.float32)
        inverse = 1.0 / (jnp.sqrt(re * re + im * im) + WATER)
        re = (re * inverse).astype(jnp.bfloat16)
        im = (im * inverse).astype(jnp.bfloat16)
        right[g, :128, :chans] = re
        right[g, :128, chans:] = im
        right[g, 128:, :chans] = im
        right[g, 128:, chans:] = -re
        both = jnp.concatenate([re, im], axis=0)
        got = lax.dot_general(chosen, both, (((1,), (1,)), ((), ())),
                              preferred_element_type=jnp.float32).astype(jnp.bfloat16)
        to = pl.ds(pl.multiple_of(i * 128, 128), 128)
        for u in range(steps):
            for k in range(2):
                held[u, 2 * k + h, :, to] = got[u * per_step:(u + 1) * per_step, k * 128:(k + 1) * 128]

    def repeat(count, unroll, body):
        def some(i, carry):
            for r in range(unroll):
                body(i * unroll + r)
            return carry

        lax.fori_loop(0, count // unroll, some, 0)

    for h in range(2):
        repeat(groups // 2, 4, functools.partial(prepare, h))

    pl.semaphore_wait(barrier, len(dists) + peers - 1)

    keep = 2 * bit0 + bit1
    last = len(stages) - 1

    def copy(t, st):
        d = stages[st]
        if st == 0:
            src, dst = held.at[t, pl.ds(2 * (1 - bit0), 2)], got1.at[t]
        elif st == 1:
            src, dst = held.at[t, 2 * bit0 + 1 - bit1], got2.at[t]
        elif st < last - 1:
            src, dst = held.at[t, keep], got_full.at[t, st - 2]
        elif st == last - 1:
            src = dst = whole.at[t, keep]
        else:
            src = dst = whole.at[t, pl.ds(2 * bit0, 2)]
        return pltpu.make_async_remote_copy(
            src_ref=src, dst_ref=dst, send_sem=bsend.at[t, st], recv_sem=brecv.at[t, st],
            device_id=along(d), device_id_type=MESH)

    def finish(t, st):
        copy(t, st).wait()
        if st == 0:
            for q in range(2):
                held[t, 2 * bit0 + q] = held[t, 2 * bit0 + q] + got1[t, q]
        elif st == 1:
            held[t, keep] = held[t, keep] + got2[t]
        elif st < last - 1:
            held[t, keep] = held[t, keep] + got_full[t, st - 2]
        if st == last - 2:
            whole[t, keep] = held[t, keep]

    lane = lax.broadcasted_iota(jnp.int32, (1, group, 128), 2)
    bin_of = lax.broadcasted_iota(jnp.int32, (1, group, 128), 1)
    mine = (lane // wins) == bin_of

    def spread(x):
        wide = jnp.where(mine, x[:, None, :], 0.0)
        return wide.reshape(per_step * group, 128).astype(jnp.bfloat16)

    def exchange(v):
        return pltpu.make_async_remote_copy(
            src_ref=send.at[v], dst_ref=recv.at[v], send_sem=xsend.at[v], recv_sem=xrecv.at[v],
            device_id=peer(v * piece // block + 1), device_id_type=MESH)

    def multiply(u):
        for h in range(2):
            def one(i):
                g = pl.multiple_of(i * 128, 128)
                re = whole[u, h, :, pl.ds(g, 128)].astype(jnp.float32)
                im = whole[u, 2 + h, :, pl.ds(g, 128)].astype(jnp.float32)
                left = jnp.concatenate([spread(re), spread(im)], axis=1)
                got = jnp.dot(left, right[h * (groups // 2) + i], preferred_element_type=jnp.float32)
                first = h * (bins // 2) + i * group
                for o in range(2):
                    to = pl.ds(pl.multiple_of(o * bins + first, group), group)
                    value = got[:, o * chans:(o + 1) * chans]
                    cross[:, to, :] = value.reshape(per_step, group, chans).astype(jnp.bfloat16)

            repeat(groups // 2, 2, one)

    def lag_pair(s):
        both = jnp.concatenate([cross[s], cross[s + 1]], axis=1)
        return jnp.dot(table_ref[...], both, preferred_element_type=jnp.float32)

    def compute(u):
        multiply(u)
        for n in range(per_step // piece):
            v = u * (per_step // piece) + n

            def pair(i):
                got = lag_pair(n * piece + 2 * i)
                for r in range(2):
                    value = got[:, r * chans:(r + 1) * chans]
                    if v < sends:
                        send[v, 2 * i + r] = value.astype(jnp.bfloat16)
                    else:
                        own[(v - sends) * piece + 2 * i + r] = value

            repeat(piece // 2, min(2, piece // 2), pair)
            if v < sends:
                exchange(v).start()

    def close(w):
        for p in range(1, peers):
            exchange((p - 1) * (block // piece) + w).wait()

        def one(j):
            value = own[w * piece + j]
            for p in range(1, peers):
                value = value + recv[(p - 1) * (block // piece) + w, j].astype(jnp.float32)
            out_ref[w * piece + j] = value.T

        repeat(piece, 2, one)

    count = len(stages)
    for t in range(steps):
        copy(t, 0).start()
    for wave in range(steps + count):
        for t in range(steps):
            st = wave - t
            if 0 <= st < count:
                finish(t, st)
                if st + 1 < count:
                    copy(t, st + 1).start()
            elif st == count:
                compute(t)
    for w in range(block // piece):
        close(w)


def per_device(spectra, owners, source_rows):
    _, bins, wins, chans = spectra.shape
    steps, per_step = source_rows.shape
    n_chan, n_tm, n_freq = (lax.axis_size(a) for a in AXES[1:])
    peers = n_tm * n_freq
    per = per_step // peers
    lanes = bins * wins
    full = jnp.asarray(table(bins * n_freq, 1.0 / (wins * n_tm)).astype(jnp.bfloat16))
    tables = lax.dynamic_slice_in_dim(full, lax.axis_index("freq") * bins, bins, 2) if n_freq > 1 else full
    tables = tables.reshape(LAGS, 2 * bins)
    far = max(n_chan.bit_length() - 3, 1)
    count = n_chan.bit_length() + 1
    sizes = (steps, per_step, bins, wins, chans, n_chan, n_tm, n_freq)
    bf16, f32 = jnp.bfloat16, jnp.float32
    quarter = (per_step, lanes // 2)
    vmem = pl.BlockSpec(memory_space=pltpu.VMEM)
    smem = pl.BlockSpec(memory_space=pltpu.SMEM)
    block, piece, sends = layout(steps, per_step, peers)
    out = pl.pallas_call(
        functools.partial(kernel, sizes),
        out_shape=jax.ShapeDtypeStruct((block, chans, LAGS), f32),
        in_specs=[smem, smem, vmem, vmem],
        out_specs=vmem,
        scratch_shapes=[
            pltpu.VMEM((steps * per_step, chans), f32),
            pltpu.VMEM((lanes // 128, 256, 2 * chans), bf16),
            pltpu.VMEM((steps, 4) + quarter, bf16),
            pltpu.VMEM((steps, 2) + quarter, bf16),
            pltpu.VMEM((steps,) + quarter, bf16),
            pltpu.VMEM((steps, far) + quarter, bf16),
            pltpu.VMEM((steps, 4) + quarter, bf16),
            pltpu.VMEM((per_step, 2 * bins, chans), bf16),
            pltpu.VMEM((block, LAGS, chans), f32),
            pltpu.VMEM((max(sends, 1), piece, LAGS, chans), bf16),
            pltpu.VMEM((max(sends, 1), piece, LAGS, chans), bf16),
            pltpu.SemaphoreType.DMA((steps, count)),
            pltpu.SemaphoreType.DMA((steps, count)),
            pltpu.SemaphoreType.DMA((max(sends, 1),)),
            pltpu.SemaphoreType.DMA((max(sends, 1),)),
        ],
        compiler_params=pltpu.CompilerParams(collective_id=0, has_side_effects=True),
    )(owners, source_rows, spectra.reshape(2, lanes, chans), tables)
    return out.reshape(steps, per, chans, LAGS)


def solution(mesh):
    placed = (P(None, "freq", "tm", ("parts", "chan")), P("parts"), P("parts", None))
    return jax.shard_map(
        per_device,
        mesh=mesh,
        in_specs=placed,
        out_specs=P(None, ("tm", "freq"), ("parts", "chan"), None),
        check_vma=False,
    )
```

time: 98.4 us -> 60.3 us (0.61)
  Pallas kernels: 92.8 us -> 56.9 us
  other arithmetic: 2.1 us -> 0 us
    pallas_call x1, Pallas kernels: 92.8 us -> 56.9 us  [per_device(): pl.pallas_call(functools.partial(kernel, sizes), out_shape=jax.ShapeDtype...]
where the time goes in v2:
time: 60.3 us; the launch traced here: 60.1 us
  Pallas kernels  56.9 us (94%)
  local copies, waits for them, and re-layouts  3.14 us (5%)
    pallas_call x1, Pallas kernels, per_device(): pl.pallas_call(functools.partial(kernel, sizes), out_shape=jax.ShapeDtype...  56.9 us
    unnamed x1, local copies, waits for them, and re-layouts  3.14 us

profile of v2, /device:TPU:0, one launch (start us, length us, event | category | flops | bytes accessed | tf_op | source)
XLA Modules:
  0.0 60.1 jit_solution(2735210469089325992)
XLA Ops:
  0.0 56.9 %shard_map.46 = f32[32,128,128]{2,1,0:T(8,128)} custom-call(s32[4]{0:T(128)} %owner_ref.1, s32[4,16]{1,0:T(4,128)} %row_ref.1, bf16[2,4096,128]{2,1,0:T(8,128)(2,1)} %bitcast.3, bf16[128,1024]{1,0:T(8,128)(2,1)} %constant.3.table_ref), custom_call_target="tpu_custom_call" | custom-call | tf_op jit(solution)/shard_map/pallas_call | solution.py:237
  57.0 3.1 %copy.6 = f32[4,8,128,128]{3,2,1,0:T(8,128)} copy(f32[4,8,128,128]{3,2,1,0:T(8,128)} %bitcast.2) | data formatting | bytes 4194304

commit v3 on v2

--- a/solution.py
+++ b/solution.py
@@ -150,29 +150,30 @@
             src_ref=send.at[v], dst_ref=recv.at[v], send_sem=xsend.at[v], recv_sem=xrecv.at[v],
             device_id=peer(v * piece // block + 1), device_id_type=MESH)
 
-    def multiply(u):
-        for h in range(2):
-            def one(i):
-                g = pl.multiple_of(i * 128, 128)
-                re = whole[u, h, :, pl.ds(g, 128)].astype(jnp.float32)
-                im = whole[u, 2 + h, :, pl.ds(g, 128)].astype(jnp.float32)
-                left = jnp.concatenate([spread(re), spread(im)], axis=1)
-                got = jnp.dot(left, right[h * (groups // 2) + i], preferred_element_type=jnp.float32)
-                first = h * (bins // 2) + i * group
-                for o in range(2):
-                    to = pl.ds(pl.multiple_of(o * bins + first, group), group)
-                    value = got[:, o * chans:(o + 1) * chans]
-                    cross[:, to, :] = value.reshape(per_step, group, chans).astype(jnp.bfloat16)
-
-            repeat(groups // 2, 2, one)
+    def multiply(u, h):
+        def one(i):
+            g = pl.multiple_of(i * 128, 128)
+            re = whole[u, h, :, pl.ds(g, 128)].astype(jnp.float32)
+            im = whole[u, 2 + h, :, pl.ds(g, 128)].astype(jnp.float32)
+            left = jnp.concatenate([spread(re), spread(im)], axis=1)
+            got = jnp.dot(left, right[h * (groups // 2) + i], preferred_element_type=jnp.float32)
+            first = h * (bins // 2) + i * group
+            for o in range(2):
+                to = pl.ds(pl.multiple_of(o * bins + first, group), group)
+                value = got[:, o * chans:(o + 1) * chans]
+                cross[:, to, :] = value.reshape(per_step, group, chans).astype(jnp.bfloat16)
+
+        repeat(groups // 2, 2, one)
 
     def lag_pair(s):
         both = jnp.concatenate([cross[s], cross[s + 1]], axis=1)
         return jnp.dot(table_ref[...], both, preferred_element_type=jnp.float32)
 
-    def compute(u):
-        multiply(u)
-        for n in range(per_step // piece):
+    def compute(u, part_of):
+        if part_of < 2:
+            multiply(u, part_of)
+        else:
+            n = part_of - 2
             v = u * (per_step // piece) + n
 
             def pair(i):
@@ -200,18 +201,40 @@
 
         repeat(piece, 2, one)
 
-    count = len(stages)
+    parts_of = 2 + per_step // piece
+    urgent = -(-sends // (per_step // piece))
+    wait_of = [1.6 if d == 1 else 3.2 if d < 8 else 5.2 for d in stages]
+    now, ready, stage_of = 0.0, {}, {}
+    done = [0] * steps
+    later = []
     for t in range(steps):
-        copy(t, 0).start()
-    for wave in range(steps + count):
-        for t in range(steps):
-            st = wave - t
-            if 0 <= st < count:
-                finish(t, st)
-                if st + 1 < count:
-                    copy(t, st + 1).start()
-            elif st == count:
-                compute(t)
+        if t < max(urgent, 1):
+            copy(t, 0).start()
+            ready[t], stage_of[t] = wait_of[0] * (t + 1), 0
+        else:
+            later.append(t)
+    while any(n < parts_of for n in done):
+        if later and now >= sum(wait_of[:3]):
+            for t in later:
+                copy(t, 0).start()
+                ready[t], stage_of[t] = now + wait_of[0] * (t + 1 - later[0]), 0
+            later = []
+        due = [t for t in ready if ready[t] <= now]
+        todo = [t for t in range(steps) if stage_of.get(t) == len(stages) and done[t] < parts_of]
+        if not due and todo:
+            compute(todo[0], done[todo[0]])
+            now += 2.2 if done[todo[0]] < 2 else 0.7
+            done[todo[0]] += 1
+        else:
+            t = due[0] if due else min(ready, key=lambda i: ready[i])
+            now = max(now, ready[t])
+            finish(t, stage_of[t])
+            stage_of[t] += 1
+            if stage_of[t] < len(stages):
+                copy(t, stage_of[t]).start()
+                ready[t] = now + wait_of[stage_of[t]]
+            else:
+                del ready[t]
     for w in range(block // piece):
         close(w)
 

time: 60.3 us -> 62 us (1.028)
  Pallas kernels: 56.9 us -> 58.7 us
    pallas_call x1, Pallas kernels: 56.9 us -> 58.7 us  [per_device(): pl.pallas_call(functools.partial(kernel, sizes), out_shape=jax.ShapeDtype...]
where the time goes in v3:
time: 62 us; the launch traced here: 61.9 us
  Pallas kernels  58.7 us (95%)
  local copies, waits for them, and re-layouts  3.14 us (5%)
    pallas_call x1, Pallas kernels, per_device(): pl.pallas_call(functools.partial(kernel, sizes), out_shape=jax.ShapeDtype...  58.7 us
    unnamed x1, local copies, waits for them, and re-layouts  3.14 us

profile of v3, /device:TPU:0, one launch (start us, length us, event | category | flops | bytes accessed | tf_op | source)
XLA Modules:
  0.0 61.9 jit_solution(13918307235959493180)
XLA Ops:
  0.0 58.7 %shard_map.46 = f32[32,128,128]{2,1,0:T(8,128)} custom-call(s32[4]{0:T(128)} %owner_ref.1, s32[4,16]{1,0:T(4,128)} %row_ref.1, bf16[2,4096,128]{2,1,0:T(8,128)(2,1)} %bitcast.3, bf16[128,1024]{1,0:T(8,128)(2,1)} %constant.3.table_ref), custom_call_target="tpu_custom_call" | custom-call | tf_op jit(solution)/shard_map/pallas_call | solution.py:260
  58.7 3.1 %copy.6 = f32[4,8,128,128]{3,2,1,0:T(8,128)} copy(f32[4,8,128,128]{3,2,1,0:T(8,128)} %bitcast.2) | data formatting | bytes 4194304

commit v4 on v3

--- a/solution.py
+++ b/solution.py
@@ -202,23 +202,13 @@
         repeat(piece, 2, one)
 
     parts_of = 2 + per_step // piece
-    urgent = -(-sends // (per_step // piece))
     wait_of = [1.6 if d == 1 else 3.2 if d < 8 else 5.2 for d in stages]
     now, ready, stage_of = 0.0, {}, {}
     done = [0] * steps
-    later = []
     for t in range(steps):
-        if t < max(urgent, 1):
-            copy(t, 0).start()
-            ready[t], stage_of[t] = wait_of[0] * (t + 1), 0
-        else:
-            later.append(t)
+        copy(t, 0).start()
+        ready[t], stage_of[t] = wait_of[0] * (t + 1), 0
     while any(n < parts_of for n in done):
-        if later and now >= sum(wait_of[:3]):
-            for t in later:
-                copy(t, 0).start()
-                ready[t], stage_of[t] = now + wait_of[0] * (t + 1 - later[0]), 0
-            later = []
         due = [t for t in ready if ready[t] <= now]
         todo = [t for t in range(steps) if stage_of.get(t) == len(stages) and done[t] < parts_of]
         if not due and todo:

time: 62 us -> 63.9 us (1.031)
  Pallas kernels: 58.7 us -> 60.6 us
    pallas_call x1, Pallas kernels: 58.7 us -> 60.6 us  [per_device(): pl.pallas_call(functools.partial(kernel, sizes), out_shape=jax.ShapeDtype...]
where the time goes in v4:
time: 63.9 us; the launch traced here: 63.8 us
  Pallas kernels  60.6 us (95%)
  local copies, waits for them, and re-layouts  3.14 us (5%)
    pallas_call x1, Pallas kernels, per_device(): pl.pallas_call(functools.partial(kernel, sizes), out_shape=jax.ShapeDtype...  60.6 us
    unnamed x1, local copies, waits for them, and re-layouts  3.14 us

profile of v4, /device:TPU:0, one launch (start us, length us, event | category | flops | bytes accessed | tf_op | source)
XLA Modules:
  0.0 63.8 jit_solution(12813840287658694857)
XLA Ops:
  0.0 60.6 %shard_map.46 = f32[32,128,128]{2,1,0:T(8,128)} custom-call(s32[4]{0:T(128)} %owner_ref.1, s32[4,16]{1,0:T(4,128)} %row_ref.1, bf16[2,4096,128]{2,1,0:T(8,128)(2,1)} %bitcast.3, bf16[128,1024]{1,0:T(8,128)(2,1)} %constant.3.table_ref), custom_call_target="tpu_custom_call" | custom-call | tf_op jit(solution)/shard_map/pallas_call | solution.py:250
  60.6 3.1 %copy.6 = f32[4,8,128,128]{3,2,1,0:T(8,128)} copy(f32[4,8,128,128]{3,2,1,0:T(8,128)} %bitcast.2) | data formatting | bytes 4194304
